TPU v7x, 256 devices: a whole 4x4x8 slice. The times are simulated.
256 devices in a mesh: dp: 4 (over x), ctx: 16 (over z_lo, y), tensor: 4 (over z_hi, core).
Axes of the slice: x: 4, y: 4, z: 8 (z_hi: 2, z_lo: 4; z = z_hi * 4 + z_lo), core: 2. Of those that a mesh axis runs over, the one named last changes fastest.
Arguments:
- queries: bfloat16 [4, 4096, 4, 1024], P('dp', 'ctx', 'tensor'), may hold values from -120 to 120
- keys: bfloat16 [4, 4096, 4, 128], P('dp', 'ctx', 'tensor'), may hold values from -7 to 7
- values: bfloat16 [4, 4096, 4, 128], P('dp', 'ctx', 'tensor'), may hold values from -6 to 6
- student_x: bfloat16 [4, 4096, 4, 1024], P('dp', 'ctx', 'tensor'), may hold values from -12 to 12
- student_bc: bfloat16 [4, 4096, 4, 2, 128], P('dp', 'ctx', 'tensor'), may hold values from -2 to 2
- student_dt: float32 [4, 4096, 4, 16], P('dp', 'ctx', 'tensor'), may hold values from -4 to 4
- a_log: float32 [4, 16], P('tensor'), may hold values from -4 to 2
- dt_bias: float32 [4, 16], P('tensor'), may hold values from -5.5 to -3.5
- skip: float32 [4, 16], P('tensor'), may hold values from 0.5 to 1.5
Outputs:
- grad_x: bfloat16 [4, 4096, 4, 1024], P('dp', 'ctx', 'tensor')
- grad_bc: bfloat16 [4, 4096, 4, 2, 128], P('dp', 'ctx', 'tensor')
- grad_dt: float32 [4, 4096, 4, 16], P('dp', 'ctx', 'tensor')
- grad_heads: float32 [3, 4, 16], P(None, 'tensor')
- loss: float32 [], replicated
All inputs are finite; a program needn't handle non-finite values.
Results may differ from a plain program's by a relative error of at most 0.006.
Values may be sent and summed in bfloat16 or wider, within the bound.
A program may use at most 64 MiB of HBM per device.

v0:
```python
import jax
import jax.numpy as jnp
from jax import lax
from jax.experimental import pallas as pl
from jax.experimental.pallas import tpu as pltpu
from jax.sharding import PartitionSpec as P

T = 256
HD = 128
GROUP = 8
N = 128
HG = 16
CH = 1024
QW = 256
ROW = 4
F32 = jnp.float32
BF16 = jnp.bfloat16
NEGATIVE = -1e30
EPSILON = 1e-06
EXP_SCALE = 1.4426950408889634 * HD**-0.5
MESH = pl.DeviceIdType.MESH


def nn(a, b):
    return lax.dot_general(a, b, (((1,), (0,)), ((), ())), preferred_element_type=F32)


def nt(a, b):
    return lax.dot_general(a, b, (((1,), (1,)), ((), ())), preferred_element_type=F32)


def tn(a, b):
    return lax.dot_general(a, b, (((0,), (0,)), ((), ())), preferred_element_type=F32)


def pieces(a, count):
    out = []
    for _ in range(count - 1):
        top = a.astype(BF16)
        out.append(top)
        a = a - top.astype(F32)
    out.append(a.astype(BF16))
    return out


def summed(form, values, marks, count=3, left=True):
    total = None
    for part in pieces(values, count):
        term = form(part, marks) if left else form(marks, part)
        total = term if total is None else total + term
    return total


def iota(shape, dim):
    return lax.broadcasted_iota(jnp.int32, shape, dim)


def marks(shape, test):
    return jnp.where(test(iota(shape, 0), iota(shape, 1)), 1.0, 0.0).astype(BF16)


def column(ref):
    wide = jnp.broadcast_to(ref[...], (HG, HG))
    same = iota((HG, HG), 0) == iota((HG, HG), 1)
    return jnp.sum(jnp.where(same, wide, 0.0), axis=1, keepdims=True)


def kernel(
    entries, dp_size, tensor_size,
    q, k, v, x, bc, dt, alog, dtb, skp,
    gx, gbc, gdt, ghd, gls,
    kbuf, vbuf, m_ref, acc, timed, mixt, cumb, stepb, cumt, stept, wmat, wtmat,
    intra, inter, upb, ups, ts_full, ecum_full, xs, eu, t1,
    tot, tq,
    ysend, yrecv, zsend, zrecv, bsend, brecv,
    ysend2, yrecv2, zsend2, zrecv2, bsend2, brecv2,
    sy, sz, sd, st, hy, hz, hd,
    own_sem, kv_recv, kvz_send, kvy_send,
    tot_send, tot_recv, scan_send, scan_recv, red_send, red_recv,
):
    c = lax.axis_index("ctx")
    d = lax.axis_index("dp")
    tt = lax.axis_index("tensor")
    z = c // ROW
    y = c % ROW

    def at_y(step):
        return {"ctx": z * ROW + (y + step) % ROW}

    def at_z(step):
        return {"ctx": ((z + step) % ROW) * ROW + y}

    def at_d(step):
        return {"dp": (d + step) % dp_size}

    def at_t(step):
        return {"tensor": (tt + step) % tensor_size}

    peers = [at_y(s) for s in range(1, ROW)] + [at_z(s) for s in range(1, ROW)]
    peers += [at_d(s) for s in range(1, dp_size)] + [at_t(s) for s in range(1, tensor_size)]

    zrecv[...] = jnp.zeros_like(zrecv)
    zrecv2[...] = jnp.zeros_like(zrecv2)

    barrier = pltpu.get_barrier_semaphore()
    for peer in peers:
        pl.semaphore_signal(barrier, inc=1, device_id=peer, device_id_type=MESH)

    def rows(slot):
        return pl.ds(pl.multiple_of(slot * T, T), T)

    own_k = pltpu.make_async_copy(k, kbuf.at[rows(c)], own_sem.at[0])
    own_v = pltpu.make_async_copy(v, vbuf.at[rows(c)], own_sem.at[1])
    own_k.start()
    own_v.start()
    pl.semaphore_wait(barrier, len(peers))

    def remote(src, dst, send, recv, peer):
        return pltpu.make_async_remote_copy(
            src_ref=src, dst_ref=dst, send_sem=send, recv_sem=recv,
            device_id=peer, device_id_type=MESH,
        )

    bufs = (kbuf, vbuf)

    def kv_z(step, which):
        return remote(
            (k, v)[which], bufs[which].at[rows(c)], kvz_send.at[step - 1, which],
            kv_recv.at[which, c], at_z(step),
        )

    def kv_y(back, lane, which, slot, step):
        return remote(
            bufs[which].at[rows(slot)], bufs[which].at[rows(slot)], kvy_send.at[back, lane],
            kv_recv.at[which, slot], at_y(step),
        )

    def kv_wait(which, slot):
        remote(
            bufs[which].at[rows(slot)], bufs[which].at[rows(slot)], own_sem.at[which],
            kv_recv.at[which, slot], at_y(1),
        ).wait_recv()

    def y_sends(back):
        slot = (z - back) * ROW + y
        return [
            kv_y(back, 0, 0, slot, 1), kv_y(back, 1, 1, slot, 3),
            kv_y(back, 2, 1, slot, 1), kv_y(back, 3, 0, slot, 3),
        ]

    def slot_of(back, step):
        return (z - back) * ROW + (y + step) % ROW

    def forwards(back):
        return [kv_y(back, 4, 0, slot_of(back, 3), 1), kv_y(back, 5, 1, slot_of(back, 1), 3)]

    for step in (3, 2, 1):

        @pl.when(z + step < ROW)
        def _():
            for which in range(2):
                kv_z(step, which).start()

    own_k.wait()
    own_v.wait()
    for copy in y_sends(0):
        copy.start()

    def pass_down(back):
        for which in range(2):
            kv_wait(which, slot_of(back, 0))
        for copy in y_sends(back):
            copy.start()

    def pass_on(back):
        kv_wait(0, slot_of(back, 3))
        kv_wait(1, slot_of(back, 1))
        for copy in forwards(back):
            copy.start()

    def settle(back):
        kv_wait(1, slot_of(back, 3))
        kv_wait(0, slot_of(back, 1))
        for which in range(2):
            kv_wait(which, slot_of(back, 2))

    bias = column(dtb)
    rate = jnp.exp(column(alog))
    shifted = dt[...] + bias
    step_size = jnp.maximum(shifted, 0.0) + jnp.log1p(jnp.exp(-jnp.abs(shifted)))
    decay = -step_size * rate
    upto = marks((T, T), lambda s, t: s <= t)
    same = marks((T, T), lambda s, t: s == t)
    cum_t = summed(nn, decay, upto)
    cum_c = summed(nt, cum_t, same, left=False)
    total = cum_t[:, T - 1 : T]
    cumt[...] = cum_t
    stept[...] = step_size
    spread = marks((HG, CH), lambda h, j: (j >> 6) == h)
    tail_step = jnp.exp(total - cum_t) * step_size
    ts_full[...] = summed(tn, tail_step, spread, 2)
    xs[...] = (ts_full[...] * x[...].astype(F32)).astype(BF16)
    pick_b = marks((T, 2 * T), lambda t, r: r == 2 * t)
    pick_c = marks((T, 2 * T), lambda t, r: r == 2 * t + 1)
    b_f = nn(pick_b, bc[...])
    c_f = nn(pick_c, bc[...])
    b_rows = b_f.astype(BF16)
    c_rows = c_f.astype(BF16)
    b_cols = b_f.T.astype(BF16)
    c_cols = c_f.T.astype(BF16)

    tot[pl.ds(c, 1)] = jnp.broadcast_to(
        jnp.concatenate([cum_c[T - 1 : T, :], jnp.zeros((1, 128 - HG), F32)], axis=1)[None],
        (1, 8, 128),
    )
    for part in range(4):
        ysend[part] = nn(b_cols, xs[:, part * QW : (part + 1) * QW]).astype(BF16)

    def tot_y(step):
        return remote(
            tot.at[pl.ds(c, 1)], tot.at[pl.ds(c, 1)], tot_send.at[0, step - 1],
            tot_recv.at[0, y], at_y(step),
        )

    def tot_y_wait(step):
        other = (y + step) % ROW
        remote(
            tot.at[pl.ds(c, 1)], tot.at[pl.ds(z * ROW + other, 1)], tot_send.at[0, step - 1],
            tot_recv.at[0, other], at_y(step),
        ).wait_recv()

    def tot_z(step):
        return remote(
            tot.at[pl.ds(z * ROW, ROW)], tot.at[pl.ds(z * ROW, ROW)], tot_send.at[1, step - 1],
            tot_recv.at[1, z], at_z(step),
        )

    def tot_z_wait(step):
        other = (z + step) % ROW
        remote(
            tot.at[pl.ds(z * ROW, ROW)], tot.at[pl.ds(other * ROW, ROW)], tot_send.at[1, step - 1],
            tot_recv.at[1, other], at_z(step),
        ).wait_recv()

    def trade(phase, src, dst, step):
        to = (y + step) % ROW
        return remote(
            src.at[to], dst.at[y], scan_send.at[phase, step - 1], scan_recv.at[phase, y], at_y(step)
        )

    def trade_wait(phase, src, dst, step):
        other = (y + step) % ROW
        remote(
            src.at[other], dst.at[other], scan_send.at[phase, step - 1],
            scan_recv.at[phase, other], at_y(step),
        ).wait_recv()

    def climb(phase, src, dst, step):
        return remote(src, dst.at[z], scan_send.at[phase, step - 1], scan_recv.at[phase, z], at_z(step))

    def climb_wait(phase, src, dst, step):
        other = (z + step) % ROW
        remote(
            src, dst.at[other], scan_send.at[phase, step - 1], scan_recv.at[phase, other], at_z(step)
        ).wait_recv()

    for step in range(1, ROW):
        tot_y(step).start()
    for step in range(1, ROW):
        trade(0, ysend, yrecv, step).start()
    yrecv[pl.ds(y, 1)] = ysend[pl.ds(y, 1)]

    wmat[...] = nt(c_rows, b_rows)
    wtmat[...] = nt(b_rows, c_rows)
    wide = marks((HG, HG * 128), lambda h, j: (j >> 7) == h)
    cumb[...] = summed(tn, cum_t, wide)
    stepb[...] = summed(tn, step_size, wide)
    ecum_full[...] = summed(tn, jnp.exp(cum_t), spread, 2)

    for step in range(1, ROW):
        tot_y_wait(step)
    for step in range(1, ROW):
        tot_z(step).start()

    low_half = iota((T, 128), 1) < 64
    zero_pair = jnp.zeros((T, 128), BF16)

    def halves(pair):
        return jnp.where(low_half, pair, zero_pair), jnp.where(low_half, zero_pair, pair)

    def lanes(index, width):
        return pl.ds(pl.multiple_of(index * width, width), width)

    def mix_pair(pair, carry):
        lower = iota((T, T), 0) >= iota((T, T), 1)
        upper = iota((T, T), 0) <= iota((T, T), 1)
        parts = halves(x[:, lanes(pair, 128)])
        result = jnp.zeros((T, 128), F32)
        for i in range(2):
            h = 2 * pair + i
            at_t = cumb[:, lanes(h, 128)]
            at_t = jnp.concatenate([at_t, at_t], axis=1)
            size_c = stepb[:, lanes(h, 128)]
            size_c = jnp.concatenate([size_c, size_c], axis=1)
            at_s = cumt[pl.ds(h, 1), :]
            size_r = stept[pl.ds(h, 1), :]
            held = jnp.exp(jnp.where(lower, at_t - at_s, NEGATIVE)) * size_r
            timed[h] = held
            mixed = (held * wmat[...]).astype(BF16)
            result = result + nn(mixed, parts[i])
            turned = jnp.exp(jnp.where(upper, at_s - at_t, NEGATIVE)) * size_c
            mixt[h] = (turned * wtmat[...]).astype(BF16)
        intra[:, lanes(pair, 128)] = result
        return carry

    @pl.when(z >= 1)
    def _():
        pass_down(1)

    lax.fori_loop(0, GROUP, mix_pair, 0)
    pass_on(0)

    tot_all_ready = [tot_z_wait(step) for step in range(1, ROW)]
    del tot_all_ready
    totals = jnp.sum(jnp.where(iota((16, 8, 128), 1) == 0, tot[...], 0.0), axis=1)
    mine = marks((128, QW), lambda h, j: h == y * 4 + (j >> 6))
    tq[...] = summed(nn, totals, mine)

    def total_of(zz, kk):
        return tq[pl.ds(zz * ROW + kk, 1), :]

    def row_total(zz):
        return total_of(zz, 0) + total_of(zz, 1) + total_of(zz, 2) + total_of(zz, 3)

    def scan_row(phase, src, got, up, order):
        for step in range(1, ROW):
            trade_wait(phase, src, got, step)
        run = jnp.zeros((N, QW), F32)
        before = {}
        for kk in order:
            before[kk] = run
            run = jnp.exp(total_of(z, kk)) * run + got[kk].astype(F32)
        up[...] = run.astype(BF16)
        return before

    def scan_back(phase, got, back, final, before, order, rows_in, arrived):
        held = jnp.zeros((N, QW), F32)
        for zz in rows_in:
            held = jnp.where(
                arrived(zz), jnp.exp(row_total(zz)) * held + got[zz].astype(F32), held
            )
        passed = jnp.zeros((1, QW), F32)
        for kk in order:
            back[kk] = (jnp.exp(passed) * held + before[kk]).astype(BF16)
            passed = passed + total_of(z, kk)
        for step in range(1, ROW):
            trade(phase, back, final, step).start()
        final[pl.ds(y, 1)] = back[pl.ds(y, 1)]

    ahead = (0, 1, 2, 3)
    behind = (3, 2, 1, 0)
    before = scan_row(0, ysend, yrecv, zsend, ahead)
    for step in range(1, ROW):

        @pl.when(z + step < ROW)
        def _():
            climb(1, zsend, zrecv, step).start()

    ones = jnp.ones((ROW * T, HD), BF16)

    def attend(back, first):
        base = pl.multiple_of((z - back) * (ROW * T), ROW * T)

        def one(g, carry):
            keys = kbuf[pl.ds(base, ROW * T), :]
            both = jnp.concatenate([vbuf[pl.ds(base, ROW * T), :], ones], axis=1)
            scores = nt(q[:, lanes(g, HD)], keys)
            if first:
                seen = iota((T, ROW * T), 1) <= iota((T, ROW * T), 0) + y * T
                scores = jnp.where(seen, scores, NEGATIVE)
            top = jnp.max(scores, axis=1, keepdims=True)
            if first:
                new = jnp.broadcast_to(top, (T, HD))
            else:
                old = m_ref[g]
                new = jnp.maximum(old, top)
            weights = jnp.exp2((scores - jnp.concatenate([new] * 8, axis=1)) * EXP_SCALE)
            part = nn(weights.astype(BF16), both)
            if first:
                acc[g] = part
            else:
                scale = jnp.exp2((old - new) * EXP_SCALE)
                acc[g] = acc[g] * jnp.concatenate([scale, scale], axis=1) + part
            m_ref[g] = new
            return carry

        lax.fori_loop(0, GROUP, one, 0)

    @pl.when(z >= 2)
    def _():
        pass_down(2)

    settle(0)
    attend(0, True)

    @pl.when(z >= 1)
    def _():
        pass_on(1)

    for step in range(1, ROW):

        @pl.when(z >= step)
        def _():
            climb_wait(1, zsend, zrecv, ROW - step)

    scan_back(2, zrecv, bsend, brecv, before, ahead, (0, 1, 2), lambda zz: zz < z)

    @pl.when(z >= 3)
    def _():
        pass_down(3)

    @pl.when(z >= 1)
    def _():
        settle(1)
        attend(1, False)

    @pl.when(z >= 2)
    def _():
        pass_on(2)

    @pl.when(z >= 3)
    def _():
        pass_on(3)

    for step in range(1, ROW):
        trade_wait(2, bsend, brecv, step)
    for part in range(4):
        cut = slice(part * QW, (part + 1) * QW)
        inter[:, cut] = ecum_full[:, cut] * nn(c_rows, brecv[part])

    for back in (2, 3):

        @pl.when(z >= back)
        def _():
            settle(back)
            attend(back, False)

    skip_row = summed(nn, jnp.broadcast_to(skp[...], (8, HG)), spread)[0:1, :]

    def fold(a):
        a = a.reshape(T // 8, 8, a.shape[1])
        a = jnp.sum(a, axis=0)
        out = a[:, 0:128]
        for j in range(1, a.shape[1] // 128):
            out = out + a[:, j * 128 : (j + 1) * 128]
        return out

    power = jnp.zeros((8, 128), F32)
    error = jnp.zeros((8, 128), F32)
    for g in range(GROUP):
        cut = slice(g * 128, (g + 1) * 128)
        both = acc[g]
        goal = (both[:, :HD] / both[:, HD:]).astype(BF16).astype(F32)
        made = intra[:, cut] + inter[:, cut] + skip_row[:, cut] * x[:, cut].astype(F32)
        resid = made - goal
        power = power + fold(goal * goal)
        error = error + fold(resid * resid)
        up = 2.0 * resid
        ups[:, cut] = up
        upb[:, cut] = up.astype(BF16)
        eu[:, cut] = (ecum_full[:, cut] * up).astype(BF16)
    for part in range(4):
        ysend2[part] = nn(c_cols, eu[:, part * QW : (part + 1) * QW]).astype(BF16)
    for step in range(1, ROW):
        trade(3, ysend2, yrecv2, step).start()
    yrecv2[pl.ds(y, 1)] = ysend2[pl.ds(y, 1)]

    def spread_out(buf, place, stage, at, size):
        out = []
        for step in range(1, size):
            out.append(
                remote(
                    buf.at[pl.ds(place, 1)], buf.at[pl.ds(place, 1)], red_send.at[stage, step - 1],
                    red_recv.at[stage, place], at(step),
                )
            )
        return out

    def collect(buf, place, stage, at, size):
        for step in range(1, size):
            other = (place + step) % size
            remote(
                buf.at[pl.ds(place, 1)], buf.at[pl.ds(other, 1)], red_send.at[stage, step - 1],
                red_recv.at[stage, other], at(step),
            ).wait_recv()
        total = buf[0]
        for j in range(1, size):
            total = total + buf[j]
        return total

    def launch(value, buf, place, stage, at, size):
        buf[pl.ds(place, 1)] = value[None]
        for copy in spread_out(buf, place, stage, at, size):
            copy.start()

    launch(jnp.concatenate([power, error], axis=0), sy, y, 0, at_y, ROW)

    before2 = scan_row(3, ysend2, yrecv2, zsend2, behind)
    for step in range(1, ROW):

        @pl.when(z >= step)
        def _():
            climb(4, zsend2, zrecv2, ROW - step).start()

    launch(collect(sy, y, 0, at_y, ROW), sz, z, 1, at_z, ROW)

    def pair_products(pair, running):
        ups_pair = halves(upb[:, lanes(pair, 128)])
        x_pair = x[:, lanes(pair, 128)]
        through = jnp.zeros((T, 128), F32)
        for i in range(2):
            h = 2 * pair + i
            running = running + timed[h] * nt(ups_pair[i], x_pair)
            through = through + nn(mixt[h], ups_pair[i])
        t1[:, lanes(pair, 128)] = through
        return running

    paired = lax.fori_loop(0, GROUP // 2, pair_products, jnp.zeros((T, T), F32))
    launch(collect(sz, z, 1, at_z, ROW), sd, d, 2, at_d, dp_size)
    for step in range(1, ROW):

        @pl.when(z + step < ROW)
        def _():
            climb_wait(4, zsend2, zrecv2, step)

    scan_back(5, zrecv2, bsend2, brecv2, before2, behind, (3, 2, 1), lambda zz: zz > z)
    paired = lax.fori_loop(GROUP // 2, GROUP, pair_products, paired)
    launch(collect(sd, d, 2, at_d, dp_size), st, tt, 3, at_t, tensor_size)

    paired_rows = paired.astype(BF16)
    paired_cols = paired.T.astype(BF16)
    grad_b = nn(paired_cols, c_rows)
    grad_c = nn(paired_rows, b_rows)
    for part in range(4):
        grad_c = grad_c + nt(eu[:, part * QW : (part + 1) * QW], brecv[part])

    def by_head(a):
        return summed(nt, a, spread, 2, left=False)

    xf = x[...].astype(F32)
    gained = by_head(upb[...].astype(F32) * intra[...] - xf * t1[...]) + by_head(
        ups[...] * inter[...]
    )
    from_mix = by_head(xf * t1[...])
    skip_term = jnp.sum(by_head(ups[...] * xf), axis=1, keepdims=True)
    since = marks((T, T), lambda s, t: s >= t)
    until = marks((T, T), lambda s, t: s < t)
    gained_after = summed(nn, gained, since)
    gate = 1.0 / (1.0 + jnp.exp(-shifted))

    both_sums = collect(st, tt, 3, at_t, tensor_size)
    power_all = jnp.sum(both_sums[0:8, :], keepdims=True)
    error_all = jnp.sum(both_sums[8:16, :], keepdims=True)
    mean_square = power_all / entries + EPSILON
    factor = 1.0 / mean_square
    gls[...] = jnp.broadcast_to(error_all / mean_square / entries, (8, 128))

    for step in range(1, ROW):
        trade_wait(5, bsend2, brecv2, step)
    overlap = []
    for part in range(4):
        cut = slice(part * QW, (part + 1) * QW)
        later = brecv2[part]
        inter[:, cut] = ts_full[:, cut] * nn(b_rows, later)
        prod = later.astype(F32) * brecv[part].astype(F32)
        overlap.append(jnp.sum(prod.reshape(N // 8, 8, QW), axis=0))
    from_later = by_head(xf * inter[...])
    meet = jnp.sum(by_head(jnp.concatenate(overlap, axis=1)), axis=1, keepdims=True)
    decay_grad = gained_after + summed(nn, from_later, until) + jnp.exp(total) * meet
    direct = (from_mix + from_later) / step_size
    shift_grad = (direct - decay_grad * rate) * gate
    decay_term = jnp.sum(decay_grad * decay, axis=1, keepdims=True)
    shift_term = jnp.sum(shift_grad, axis=1, keepdims=True)
    lane = iota((HG, 128), 1)
    heads = jnp.where(lane == 0, decay_term, jnp.where(lane == 1, shift_term, skip_term))
    launch(heads, hy, y, 4, at_y, ROW)
    gdt[...] = shift_grad * factor
    for part in range(4):
        grad_b = grad_b + nt(xs[:, part * QW : (part + 1) * QW], brecv2[part])
    launch(collect(hy, y, 4, at_y, ROW), hz, z, 5, at_z, ROW)
    put_b = marks((2 * T, T), lambda r, t: r == 2 * t)
    put_c = marks((2 * T, T), lambda r, t: r == 2 * t + 1)
    gbc[...] = (
        nn(put_b, (grad_b * factor).astype(BF16)) + nn(put_c, (grad_c * factor).astype(BF16))
    ).astype(BF16)
    launch(collect(hz, z, 5, at_z, ROW), hd, d, 6, at_d, dp_size)
    gx[...] = ((skip_row * ups[...] + t1[...] + inter[...]) * factor).astype(BF16)
    ghd[...] = collect(hd, d, 6, at_d, dp_size) * factor

    for step in range(1, ROW):

        @pl.when(z + step < ROW)
        def _():
            for which in range(2):
                kv_z(step, which).wait_send()
            climb(1, zsend, zrecv, step).wait_send()

        @pl.when(z >= step)
        def _():
            climb(4, zsend2, zrecv2, ROW - step).wait_send()

        tot_y(step).wait_send()
        tot_z(step).wait_send()
        trade(0, ysend, yrecv, step).wait_send()
        trade(2, bsend, brecv, step).wait_send()
        trade(3, ysend2, yrecv2, step).wait_send()
        trade(5, bsend2, brecv2, step).wait_send()
    for back in range(ROW):

        @pl.when(z >= back)
        def _():
            for copy in y_sends(back) + forwards(back):
                copy.wait_send()

    for buf, place, stage, at, size in (
        (sy, y, 0, at_y, ROW), (sz, z, 1, at_z, ROW), (sd, d, 2, at_d, dp_size),
        (st, tt, 3, at_t, tensor_size), (hy, y, 4, at_y, ROW), (hz, z, 5, at_z, ROW),
        (hd, d, 6, at_d, dp_size),
    ):
        for copy in spread_out(buf, place, stage, at, size):
            copy.wait_send()


def solution(mesh):
    dp_size, tensor_size = mesh.shape["dp"], mesh.shape["tensor"]
    entries = float(dp_size * mesh.shape["ctx"] * tensor_size * T * CH)

    def vm(shape, kind):
        return pltpu.VMEM(shape, kind)

    chunk4 = (ROW, N, QW)
    scratch = [
        vm((16 * T, HD), BF16), vm((16 * T, HD), BF16),
        vm((GROUP, T, HD), F32), vm((GROUP, T, 2 * HD), F32),
        vm((HG, T, T), F32), vm((HG, T, T), BF16),
        vm((T, HG * 128), F32), vm((T, HG * 128), F32),
        vm((HG, T), F32), vm((HG, T), F32), vm((T, T), F32), vm((T, T), F32),
        vm((T, CH), F32), vm((T, CH), F32), vm((T, CH), BF16), vm((T, CH), F32),
        vm((T, CH), F32), vm((T, CH), F32), vm((T, CH), BF16), vm((T, CH), BF16),
        vm((T, CH), F32),
        vm((16, 8, 128), F32), vm((16, QW), F32),
    ]
    for _ in range(2):
        scratch += [
            vm(chunk4, BF16), vm(chunk4, BF16), vm((N, QW), BF16), vm(chunk4, BF16),
            vm(chunk4, BF16), vm(chunk4, BF16),
        ]
    scratch += [
        vm((ROW, 16, 128), F32), vm((ROW, 16, 128), F32), vm((dp_size, 16, 128), F32),
        vm((tensor_size, 16, 128), F32), vm((ROW, 16, 128), F32), vm((ROW, 16, 128), F32),
        vm((dp_size, 16, 128), F32),
    ]
    sem = pltpu.SemaphoreType.DMA
    scratch += [
        sem((2,)), sem((2, 16)), sem((3, 2)), sem((4, 6)),
        sem((2, 3)), sem((2, 4)), sem((6, 3)), sem((6, 4)), sem((7, 3)), sem((7, 4)),
    ]

    def body(queries, keys, values, student_x, student_bc, student_dt, a_log, dt_bias, skip):
        whole = pl.BlockSpec(memory_space=pltpu.VMEM)

        def run(*refs):
            kernel(entries, dp_size, tensor_size, *refs)

        gx, gbc, gdt, ghd, gls = pl.pallas_call(
            run,
            out_shape=(
                jax.ShapeDtypeStruct((T, CH), BF16),
                jax.ShapeDtypeStruct((2 * T, N), BF16),
                jax.ShapeDtypeStruct((HG, T), F32),
                jax.ShapeDtypeStruct((HG, 128), F32),
                jax.ShapeDtypeStruct((8, 128), F32),
            ),
            in_specs=[whole] * 9,
            out_specs=(whole,) * 5,
            scratch_shapes=scratch,
            compiler_params=pltpu.CompilerParams(
                collective_id=0, has_side_effects=True, vmem_limit_bytes=60 * 1024 * 1024
            ),
            name="align",
        )(
            queries.reshape(T, CH), keys.reshape(T, HD), values.reshape(T, HD),
            student_x.reshape(T, CH), student_bc.reshape(2 * T, N),
            student_dt.reshape(T, HG).T, a_log, dt_bias, skip,
        )
        return (
            gx.reshape(1, T, 1, CH),
            gbc.reshape(1, T, 1, 2, N),
            gdt.T.reshape(1, T, 1, HG),
            ghd[:, :3].T.reshape(3, 1, HG),
            gls[0, 0],
        )

    return jax.shard_map(
        body,
        mesh=mesh,
        in_specs=(
            P("dp", "ctx", "tensor", None),
            P("dp", "ctx", "tensor", None),
            P("dp", "ctx", "tensor", None),
            P("dp", "ctx", "tensor", None),
            P("dp", "ctx", "tensor", None, None),
            P("dp", "ctx", "tensor", None),
            P("tensor", None),
            P("tensor", None),
            P("tensor", None),
        ),
        out_specs=(
            P("dp", "ctx", "tensor", None),
            P("dp", "ctx", "tensor", None, None),
            P("dp", "ctx", "tensor", None),
            P(None, "tensor", None),
            P(),
        ),
        check_vma=False,
    )
```

profile of v0, /device:TPU:32, one launch (start us, length us, event | category | flops | bytes accessed | tf_op | source)
XLA Modules:
  0.0 103.4 jit_solution(7558693794575244295)
XLA Ops:
  0.6 97.0 %align.1 = (bf16[256,1024]{1,0:T(8,128)(2,1)}, bf16[512,128]{1,0:T(8,128)(2,1)}, f32[16,256]{1,0:T(8,128)}, f32[16,128]{1,0:T(8,128)}, f32[8,128]{1,0:T(8,128)}) custom-call(bf16[256,1024]{1,0:T(8,128)(2,1)} %bitcast.20, bf16[256,128]{1,0:T(8,128)(2,1)} %bitcast.25, bf16[256,128]{1,0:T(8,128)(2,1)} %bitcast.26, bf16[256,1024]{1,0:T(8,128)(2,1)} %bitcast.21, ...), custom_call_target="tpu_custom_call" | custom-call | tf_op jit(solution)/shard_map/align/pallas_call | solution.py:675
  97.6 1.2 %slice.7 = f32[1,1]{1,0:T(1,128)} slice(f32[8,128]{1,0:T(8,128)} %get-tuple-element.14), slice={[0:1], [0:1]} | slice | bytes 8 | tf_op jit(solution)/shard_map/slice | solution.py:701
  98.8 0.0 copy-start.2
  98.8 0.7 copy-done.2
  99.5 0.6 copy.16
  100.1 0.0 copy-start
  100.1 1.9 %copy.22 = bf16[1,256,1,1024]{3,1,2,0:T(8,128)(2,1)} copy(bf16[1,256,1,1024]{3,1,2,0:T(8,128)(2,1)} %bitcast.22) | data formatting | bytes 1048576
  102.1 0.0 copy-done
  102.1 0.0 copy-start.1
  102.1 0.7 copy.23
  102.7 0.1 copy-done.1
  102.8 0.6 copy.24
  (1 shorter events, 0.0 us)
Async XLA Ops:
  98.8 0.7 copy-start.2
  100.1 1.9 %copy-start = (bf16[512,128]{1,0:T(8,128)(2,1)S(1)}, bf16[512,128]{1,0:T(8,128)(2,1)}, u32[]{:S(2)}) copy-start(bf16[512,128]{1,0:T(8,128)(2,1)} %get-tuple-element.11) | copy-start | bytes 393220
  102.1 0.7 copy-start.1
where the time goes:
time: 104 us; the launch traced here: 103 us
  Pallas kernels  97 us (93%)
  local copies, waits for them, and re-layouts  5.74 us (6%)
    pallas_call x1, Pallas kernels, body(): pl.pallas_call(run, out_shape=(jax.ShapeDtypeStruct((T, CH), BF16), jax.S...  97 us
    unnamed x10, local copies, waits for them, and re-layouts  4.56 us

commit v1 on v0

--- a/solution.py
+++ b/solution.py
@@ -67,11 +67,11 @@
 
 def kernel(
     entries, dp_size, tensor_size,
-    q, k, v, x, bc, dt, alog, dtb, skp,
+    q_in, k, v, x_in, bc_in, dt_in, alog, dtb, skp,
     gx, gbc, gdt, ghd, gls,
-    kbuf, vbuf, m_ref, acc, timed, mixt, cumb, stepb, cumt, stept, wmat, wtmat,
+    q, x, bc, dt, kbuf, vbuf, m_ref, acc, timed, mixt, cumb, stepb, cumt, stept, wmat, wtmat,
     intra, inter, upb, ups, ts_full, ecum_full, xs, eu, t1,
-    tot, tq,
+    tot, tq, before,
     ysend, yrecv, zsend, zrecv, bsend, brecv,
     ysend2, yrecv2, zsend2, zrecv2, bsend2, brecv2,
     sy, sz, sd, st, hy, hz, hd,
@@ -111,8 +111,12 @@
 
     own_k = pltpu.make_async_copy(k, kbuf.at[rows(c)], own_sem.at[0])
     own_v = pltpu.make_async_copy(v, vbuf.at[rows(c)], own_sem.at[1])
-    own_k.start()
-    own_v.start()
+    loads = [
+        pltpu.make_async_copy(src, dst, own_sem.at[2 + i])
+        for i, (src, dst) in enumerate(((dt_in, dt), (bc_in, bc), (x_in, x), (q_in, q)))
+    ]
+    for copy in [own_k, own_v] + loads:
+        copy.start()
     pl.semaphore_wait(barrier, len(peers))
 
     def remote(src, dst, send, recv, peer):
@@ -184,6 +188,12 @@
         for which in range(2):
             kv_wait(which, slot_of(back, 2))
 
+    def group_cut(part, sub):
+        g = 2 * part + sub
+        return slice(g * 128, (g + 1) * 128)
+
+    for copy in loads[:3]:
+        copy.wait()
     bias = column(dtb)
     rate = jnp.exp(column(alog))
     shifted = dt[...] + bias
@@ -213,8 +223,9 @@
         jnp.concatenate([cum_c[T - 1 : T, :], jnp.zeros((1, 128 - HG), F32)], axis=1)[None],
         (1, 8, 128),
     )
-    for part in range(4):
-        ysend[part] = nn(b_cols, xs[:, part * QW : (part + 1) * QW]).astype(BF16)
+    for sub in range(2):
+        for part in range(4):
+            ysend[sub, part] = nn(b_cols, xs[:, group_cut(part, sub)]).astype(BF16)
 
     def tot_y(step):
         return remote(
@@ -242,45 +253,50 @@
             tot_recv.at[1, other], at_z(step),
         ).wait_recv()
 
-    def trade(phase, src, dst, step):
+    def trade(phase, sub, src, dst, step):
         to = (y + step) % ROW
         return remote(
-            src.at[to], dst.at[y], scan_send.at[phase, step - 1], scan_recv.at[phase, y], at_y(step)
+            src.at[sub, to], dst.at[sub, y], scan_send.at[phase, sub, step - 1],
+            scan_recv.at[phase, sub, y], at_y(step),
         )
 
-    def trade_wait(phase, src, dst, step):
+    def trade_wait(phase, sub, src, dst, step):
         other = (y + step) % ROW
         remote(
-            src.at[other], dst.at[other], scan_send.at[phase, step - 1],
-            scan_recv.at[phase, other], at_y(step),
+            src.at[sub, other], dst.at[sub, other], scan_send.at[phase, sub, step - 1],
+            scan_recv.at[phase, sub, other], at_y(step),
         ).wait_recv()
 
-    def climb(phase, src, dst, step):
-        return remote(src, dst.at[z], scan_send.at[phase, step - 1], scan_recv.at[phase, z], at_z(step))
-
-    def climb_wait(phase, src, dst, step):
+    def climb(phase, sub, src, dst, step):
+        return remote(
+            src.at[sub], dst.at[sub, z], scan_send.at[phase, sub, step - 1],
+            scan_recv.at[phase, sub, z], at_z(step),
+        )
+
+    def climb_wait(phase, sub, src, dst, step):
         other = (z + step) % ROW
         remote(
-            src, dst.at[other], scan_send.at[phase, step - 1], scan_recv.at[phase, other], at_z(step)
+            src.at[sub], dst.at[sub, other], scan_send.at[phase, sub, step - 1],
+            scan_recv.at[phase, sub, other], at_z(step),
         ).wait_recv()
+
+    def trades(phase, sub, src, dst):
+        for step in (2, 1, 3):
+            trade(phase, sub, src, dst, step).start()
+        dst[sub, pl.ds(y, 1)] = src[sub, pl.ds(y, 1)]
 
     for step in range(1, ROW):
         tot_y(step).start()
-    for step in range(1, ROW):
-        trade(0, ysend, yrecv, step).start()
-    yrecv[pl.ds(y, 1)] = ysend[pl.ds(y, 1)]
+    for sub in range(2):
+        trades(0, sub, ysend, yrecv)
 
     wmat[...] = nt(c_rows, b_rows)
     wtmat[...] = nt(b_rows, c_rows)
-    wide = marks((HG, HG * 128), lambda h, j: (j >> 7) == h)
-    cumb[...] = summed(tn, cum_t, wide)
-    stepb[...] = summed(tn, step_size, wide)
+    step_c = summed(nt, step_size, same, left=False)
+    for h in range(HG):
+        cumb[:, h * 128 : (h + 1) * 128] = jnp.broadcast_to(cum_c[:, h : h + 1], (T, 128))
+        stepb[:, h * 128 : (h + 1) * 128] = jnp.broadcast_to(step_c[:, h : h + 1], (T, 128))
     ecum_full[...] = summed(tn, jnp.exp(cum_t), spread, 2)
-
-    for step in range(1, ROW):
-        tot_y_wait(step)
-    for step in range(1, ROW):
-        tot_z(step).start()
 
     low_half = iota((T, 128), 1) < 64
     zero_pair = jnp.zeros((T, 128), BF16)
@@ -313,65 +329,72 @@
         intra[:, lanes(pair, 128)] = result
         return carry
 
+    lax.fori_loop(0, GROUP // 2, mix_pair, 0)
+    pass_on(0)
+
     @pl.when(z >= 1)
     def _():
         pass_down(1)
 
-    lax.fori_loop(0, GROUP, mix_pair, 0)
-    pass_on(0)
+    for step in range(1, ROW):
+        tot_y_wait(step)
+    for step in range(1, ROW):
+        tot_z(step).start()
+    lax.fori_loop(GROUP // 2, GROUP, mix_pair, 0)
 
     tot_all_ready = [tot_z_wait(step) for step in range(1, ROW)]
     del tot_all_ready
     totals = jnp.sum(jnp.where(iota((16, 8, 128), 1) == 0, tot[...], 0.0), axis=1)
     mine = marks((128, QW), lambda h, j: h == y * 4 + (j >> 6))
-    tq[...] = summed(nn, totals, mine)
-
-    def total_of(zz, kk):
-        return tq[pl.ds(zz * ROW + kk, 1), :]
-
-    def row_total(zz):
-        return total_of(zz, 0) + total_of(zz, 1) + total_of(zz, 2) + total_of(zz, 3)
-
-    def scan_row(phase, src, got, up, order):
+    here = summed(nn, totals, mine)
+    for sub in range(2):
+        tq[sub] = here[:, sub * 128 : (sub + 1) * 128]
+
+    def total_of(sub, zz, kk):
+        return tq[sub, pl.ds(zz * ROW + kk, 1), :]
+
+    def row_total(sub, zz):
+        return sum(total_of(sub, zz, kk) for kk in range(1, ROW)) + total_of(sub, zz, 0)
+
+    def scan_row(phase, sub, src, got, up, pre, order):
         for step in range(1, ROW):
-            trade_wait(phase, src, got, step)
-        run = jnp.zeros((N, QW), F32)
-        before = {}
+            trade_wait(phase, sub, src, got, step)
+        run = jnp.zeros((N, 128), F32)
         for kk in order:
-            before[kk] = run
-            run = jnp.exp(total_of(z, kk)) * run + got[kk].astype(F32)
-        up[...] = run.astype(BF16)
-        return before
-
-    def scan_back(phase, got, back, final, before, order, rows_in, arrived):
-        held = jnp.zeros((N, QW), F32)
+            pre[sub, kk] = run
+            run = jnp.exp(total_of(sub, z, kk)) * run + got[sub, kk].astype(F32)
+        up[sub] = run.astype(BF16)
+
+    def scan_back(phase, sub, got, back, final, pre, order, rows_in, arrived):
+        held = jnp.zeros((N, 128), F32)
         for zz in rows_in:
             held = jnp.where(
-                arrived(zz), jnp.exp(row_total(zz)) * held + got[zz].astype(F32), held
+                arrived(zz), jnp.exp(row_total(sub, zz)) * held + got[sub, zz].astype(F32), held
             )
-        passed = jnp.zeros((1, QW), F32)
+        passed = jnp.zeros((1, 128), F32)
         for kk in order:
-            back[kk] = (jnp.exp(passed) * held + before[kk]).astype(BF16)
-            passed = passed + total_of(z, kk)
-        for step in range(1, ROW):
-            trade(phase, back, final, step).start()
-        final[pl.ds(y, 1)] = back[pl.ds(y, 1)]
+            back[sub, kk] = (jnp.exp(passed) * held + pre[sub, kk]).astype(BF16)
+            passed = passed + total_of(sub, z, kk)
+        trades(phase, sub, back, final)
 
     ahead = (0, 1, 2, 3)
     behind = (3, 2, 1, 0)
-    before = scan_row(0, ysend, yrecv, zsend, ahead)
-    for step in range(1, ROW):
-
-        @pl.when(z + step < ROW)
-        def _():
-            climb(1, zsend, zrecv, step).start()
+    for sub in range(2):
+        scan_row(0, sub, ysend, yrecv, zsend, before, ahead)
+        for step in range(1, ROW):
+
+            @pl.when(z + step < ROW)
+            def _():
+                climb(1, sub, zsend, zrecv, step).start()
 
     ones = jnp.ones((ROW * T, HD), BF16)
 
-    def attend(back, first):
-        base = pl.multiple_of((z - back) * (ROW * T), ROW * T)
-
-        def one(g, carry):
+    def attend(row, first, heads):
+        base = pl.multiple_of(row * (ROW * T), ROW * T)
+        start, stride, count = heads
+
+        def one(i, carry):
+            g = start + stride * i
             keys = kbuf[pl.ds(base, ROW * T), :]
             both = jnp.concatenate([vbuf[pl.ds(base, ROW * T), :], ones], axis=1)
             scores = nt(q[:, lanes(g, HD)], keys)
@@ -394,56 +417,61 @@
             m_ref[g] = new
             return carry
 
-        lax.fori_loop(0, GROUP, one, 0)
+        lax.fori_loop(0, count, one, 0, unroll=4)
+
+    all_heads = (0, 1, GROUP)
+    loads[3].wait()
+    settle(0)
+    attend(z, True, (0, 2, GROUP // 2))
 
     @pl.when(z >= 2)
     def _():
         pass_down(2)
 
-    settle(0)
-    attend(0, True)
-
     @pl.when(z >= 1)
     def _():
         pass_on(1)
 
-    for step in range(1, ROW):
-
-        @pl.when(z >= step)
-        def _():
-            climb_wait(1, zsend, zrecv, ROW - step)
-
-    scan_back(2, zrecv, bsend, brecv, before, ahead, (0, 1, 2), lambda zz: zz < z)
-
     @pl.when(z >= 3)
     def _():
         pass_down(3)
 
-    @pl.when(z >= 1)
-    def _():
-        settle(1)
-        attend(1, False)
+    attend(z, True, (1, 2, GROUP // 2))
 
     @pl.when(z >= 2)
     def _():
         pass_on(2)
 
+    for sub in range(2):
+        for step in range(1, ROW):
+
+            @pl.when(z >= step)
+            def _():
+                climb_wait(1, sub, zsend, zrecv, ROW - step)
+
+        scan_back(2, sub, zrecv, bsend, brecv, before, ahead, (0, 1, 2), lambda zz: zz < z)
+
+    @pl.when(z >= 2)
+    def _():
+        settle(1)
+        attend(z - 1, False, all_heads)
+
     @pl.when(z >= 3)
     def _():
         pass_on(3)
-
-    for step in range(1, ROW):
-        trade_wait(2, bsend, brecv, step)
-    for part in range(4):
-        cut = slice(part * QW, (part + 1) * QW)
-        inter[:, cut] = ecum_full[:, cut] * nn(c_rows, brecv[part])
-
-    for back in (2, 3):
-
-        @pl.when(z >= back)
-        def _():
-            settle(back)
-            attend(back, False)
+        settle(2)
+        attend(z - 2, False, all_heads)
+
+    for sub in range(2):
+        for step in range(1, ROW):
+            trade_wait(2, sub, bsend, brecv, step)
+        for part in range(4):
+            cut = group_cut(part, sub)
+            inter[:, cut] = ecum_full[:, cut] * nn(c_rows, brecv[sub, part])
+
+    @pl.when(z >= 1)
+    def _():
+        settle(z)
 
     skip_row = summed(nn, jnp.broadcast_to(skp[...], (8, HG)), spread)[0:1, :]
 
@@ -457,23 +485,26 @@
 
     power = jnp.zeros((8, 128), F32)
     error = jnp.zeros((8, 128), F32)
-    for g in range(GROUP):
-        cut = slice(g * 128, (g + 1) * 128)
-        both = acc[g]
-        goal = (both[:, :HD] / both[:, HD:]).astype(BF16).astype(F32)
-        made = intra[:, cut] + inter[:, cut] + skip_row[:, cut] * x[:, cut].astype(F32)
-        resid = made - goal
-        power = power + fold(goal * goal)
-        error = error + fold(resid * resid)
-        up = 2.0 * resid
-        ups[:, cut] = up
-        upb[:, cut] = up.astype(BF16)
-        eu[:, cut] = (ecum_full[:, cut] * up).astype(BF16)
-    for part in range(4):
-        ysend2[part] = nn(c_cols, eu[:, part * QW : (part + 1) * QW]).astype(BF16)
-    for step in range(1, ROW):
-        trade(3, ysend2, yrecv2, step).start()
-    yrecv2[pl.ds(y, 1)] = ysend2[pl.ds(y, 1)]
+    for sub in range(2):
+
+        @pl.when(z >= 1)
+        def _():
+            attend(0, False, (sub, 2, GROUP // 2))
+
+        for part in range(4):
+            cut = group_cut(part, sub)
+            both = acc[2 * part + sub]
+            goal = (both[:, :HD] / both[:, HD:]).astype(BF16).astype(F32)
+            made = intra[:, cut] + inter[:, cut] + skip_row[:, cut] * x[:, cut].astype(F32)
+            resid = made - goal
+            power = power + fold(goal * goal)
+            error = error + fold(resid * resid)
+            up = 2.0 * resid
+            ups[:, cut] = up
+            upb[:, cut] = up.astype(BF16)
+            eu[:, cut] = (ecum_full[:, cut] * up).astype(BF16)
+            ysend2[sub, part] = nn(c_cols, eu[:, cut]).astype(BF16)
+        trades(3, sub, ysend2, yrecv2)
 
     def spread_out(buf, place, stage, at, size):
         out = []
@@ -505,12 +536,13 @@
 
     launch(jnp.concatenate([power, error], axis=0), sy, y, 0, at_y, ROW)
 
-    before2 = scan_row(3, ysend2, yrecv2, zsend2, behind)
-    for step in range(1, ROW):
-
-        @pl.when(z >= step)
-        def _():
-            climb(4, zsend2, zrecv2, ROW - step).start()
+    for sub in range(2):
+        scan_row(3, sub, ysend2, yrecv2, zsend2, before, behind)
+        for step in range(1, ROW):
+
+            @pl.when(z >= step)
+            def _():
+                climb(4, sub, zsend2, zrecv2, ROW - step).start()
 
     launch(collect(sy, y, 0, at_y, ROW), sz, z, 1, at_z, ROW)
 
@@ -527,32 +559,39 @@
 
     paired = lax.fori_loop(0, GROUP // 2, pair_products, jnp.zeros((T, T), F32))
     launch(collect(sz, z, 1, at_z, ROW), sd, d, 2, at_d, dp_size)
-    for step in range(1, ROW):
-
-        @pl.when(z + step < ROW)
-        def _():
-            climb_wait(4, zsend2, zrecv2, step)
-
-    scan_back(5, zrecv2, bsend2, brecv2, before2, behind, (3, 2, 1), lambda zz: zz > z)
     paired = lax.fori_loop(GROUP // 2, GROUP, pair_products, paired)
+    for sub in range(2):
+        for step in range(1, ROW):
+
+            @pl.when(z + step < ROW)
+            def _():
+                climb_wait(4, sub, zsend2, zrecv2, step)
+
+        scan_back(5, sub, zrecv2, bsend2, brecv2, before, behind, (3, 2, 1), lambda zz: zz > z)
     launch(collect(sd, d, 2, at_d, dp_size), st, tt, 3, at_t, tensor_size)
 
     paired_rows = paired.astype(BF16)
     paired_cols = paired.T.astype(BF16)
     grad_b = nn(paired_cols, c_rows)
     grad_c = nn(paired_rows, b_rows)
-    for part in range(4):
-        grad_c = grad_c + nt(eu[:, part * QW : (part + 1) * QW], brecv[part])
+    for sub in range(2):
+        for part in range(4):
+            grad_c = grad_c + nt(eu[:, group_cut(part, sub)], brecv[sub, part])
 
     def by_head(a):
         return summed(nt, a, spread, 2, left=False)
 
+    heads_at = marks((CH, 128), lambda j, h: (j >> 6) == h)
+    heads_next = marks((CH, 128), lambda j, h: (j >> 6) == h - HG)
     xf = x[...].astype(F32)
-    gained = by_head(upb[...].astype(F32) * intra[...] - xf * t1[...]) + by_head(
-        ups[...] * inter[...]
-    )
-    from_mix = by_head(xf * t1[...])
-    skip_term = jnp.sum(by_head(ups[...] * xf), axis=1, keepdims=True)
+    through_x = xf * t1[...]
+    gains = upb[...].astype(F32) * intra[...] - through_x + ups[...] * inter[...]
+    stats = summed(nn, gains, heads_at, 2) + nn(through_x.astype(BF16), heads_next)
+    stats = stats.T
+    gained = stats[0:HG]
+    from_mix = stats[HG : 2 * HG]
+    skip_part = jnp.sum((ups[...] * xf).reshape(T // 8, 8, CH), axis=0)
+    skip_term = jnp.sum(by_head(skip_part), axis=1, keepdims=True)
     since = marks((T, T), lambda s, t: s >= t)
     until = marks((T, T), lambda s, t: s < t)
     gained_after = summed(nn, gained, since)
@@ -565,16 +604,22 @@
     factor = 1.0 / mean_square
     gls[...] = jnp.broadcast_to(error_all / mean_square / entries, (8, 128))
 
-    for step in range(1, ROW):
-        trade_wait(5, bsend2, brecv2, step)
-    overlap = []
-    for part in range(4):
-        cut = slice(part * QW, (part + 1) * QW)
-        later = brecv2[part]
-        inter[:, cut] = ts_full[:, cut] * nn(b_rows, later)
-        prod = later.astype(F32) * brecv[part].astype(F32)
-        overlap.append(jnp.sum(prod.reshape(N // 8, 8, QW), axis=0))
-    from_later = by_head(xf * inter[...])
+    overlap = [None] * 8
+    later_stats = jnp.zeros((T, 128), F32)
+    for sub in range(2):
+        for step in range(1, ROW):
+            trade_wait(5, sub, bsend2, brecv2, step)
+        for part in range(4):
+            cut = group_cut(part, sub)
+            later = brecv2[sub, part]
+            came = ts_full[:, cut] * nn(b_rows, later)
+            inter[:, cut] = came
+            later_stats = later_stats + nn(
+                (x[:, cut].astype(F32) * came).astype(BF16), heads_at[cut, :]
+            )
+            prod = later.astype(F32) * brecv[sub, part].astype(F32)
+            overlap[2 * part + sub] = jnp.sum(prod.reshape(N // 8, 8, 128), axis=0)
+    from_later = later_stats.T[0:HG]
     meet = jnp.sum(by_head(jnp.concatenate(overlap, axis=1)), axis=1, keepdims=True)
     decay_grad = gained_after + summed(nn, from_later, until) + jnp.exp(total) * meet
     direct = (from_mix + from_later) / step_size
@@ -585,8 +630,9 @@
     heads = jnp.where(lane == 0, decay_term, jnp.where(lane == 1, shift_term, skip_term))
     launch(heads, hy, y, 4, at_y, ROW)
     gdt[...] = shift_grad * factor
-    for part in range(4):
-        grad_b = grad_b + nt(xs[:, part * QW : (part + 1) * QW], brecv2[part])
+    for sub in range(2):
+        for part in range(4):
+            grad_b = grad_b + nt(xs[:, group_cut(part, sub)], brecv2[sub, part])
     launch(collect(hy, y, 4, at_y, ROW), hz, z, 5, at_z, ROW)
     put_b = marks((2 * T, T), lambda r, t: r == 2 * t)
     put_c = marks((2 * T, T), lambda r, t: r == 2 * t + 1)
@@ -603,18 +649,21 @@
         def _():
             for which in range(2):
                 kv_z(step, which).wait_send()
-            climb(1, zsend, zrecv, step).wait_send()
+            for sub in range(2):
+                climb(1, sub, zsend, zrecv, step).wait_send()
 
         @pl.when(z >= step)
         def _():
-            climb(4, zsend2, zrecv2, ROW - step).wait_send()
+            for sub in range(2):
+                climb(4, sub, zsend2, zrecv2, ROW - step).wait_send()
 
         tot_y(step).wait_send()
         tot_z(step).wait_send()
-        trade(0, ysend, yrecv, step).wait_send()
-        trade(2, bsend, brecv, step).wait_send()
-        trade(3, ysend2, yrecv2, step).wait_send()
-        trade(5, bsend2, brecv2, step).wait_send()
+        for sub in range(2):
+            trade(0, sub, ysend, yrecv, step).wait_send()
+            trade(2, sub, bsend, brecv, step).wait_send()
+            trade(3, sub, ysend2, yrecv2, step).wait_send()
+            trade(5, sub, bsend2, brecv2, step).wait_send()
     for back in range(ROW):
 
         @pl.when(z >= back)
@@ -631,6 +680,16 @@
             copy.wait_send()
 
 
+def write_out(gx, gbc, gdt, ghd, gls, ogx, ogbc, ogdt, oghd, ogls):
+    ogx[...] = gx[...]
+    ogbc[...] = gbc[...]
+    ogdt[...] = gdt[...]
+    turned = ghd[...].T
+    for i in range(3):
+        oghd[i] = turned[i : i + 1, :]
+    ogls[...] = gls[0:1, 0:1]
+
+
 def solution(mesh):
     dp_size, tensor_size = mesh.shape["dp"], mesh.shape["tensor"]
     entries = float(dp_size * mesh.shape["ctx"] * tensor_size * T * CH)
@@ -638,8 +697,9 @@
     def vm(shape, kind):
         return pltpu.VMEM(shape, kind)
 
-    chunk4 = (ROW, N, QW)
+    chunk4 = (2, ROW, N, 128)
     scratch = [
+        vm((T, CH), BF16), vm((T, CH), BF16), vm((2 * T, N), BF16), vm((HG, T), F32),
         vm((16 * T, HD), BF16), vm((16 * T, HD), BF16),
         vm((GROUP, T, HD), F32), vm((GROUP, T, 2 * HD), F32),
         vm((HG, T, T), F32), vm((HG, T, T), BF16),
@@ -648,11 +708,11 @@
         vm((T, CH), F32), vm((T, CH), F32), vm((T, CH), BF16), vm((T, CH), F32),
         vm((T, CH), F32), vm((T, CH), F32), vm((T, CH), BF16), vm((T, CH), BF16),
         vm((T, CH), F32),
-        vm((16, 8, 128), F32), vm((16, QW), F32),
+        vm((16, 8, 128), F32), vm((2, 16, 128), F32), vm((2, ROW, N, 128), F32),
     ]
     for _ in range(2):
         scratch += [
-            vm(chunk4, BF16), vm(chunk4, BF16), vm((N, QW), BF16), vm(chunk4, BF16),
+            vm(chunk4, BF16), vm(chunk4, BF16), vm((2, N, 128), BF16), vm(chunk4, BF16),
             vm(chunk4, BF16), vm(chunk4, BF16),
         ]
     scratch += [
@@ -662,12 +722,13 @@
     ]
     sem = pltpu.SemaphoreType.DMA
     scratch += [
-        sem((2,)), sem((2, 16)), sem((3, 2)), sem((4, 6)),
-        sem((2, 3)), sem((2, 4)), sem((6, 3)), sem((6, 4)), sem((7, 3)), sem((7, 4)),
+        sem((6,)), sem((2, 16)), sem((3, 2)), sem((4, 6)),
+        sem((2, 3)), sem((2, 4)), sem((6, 2, 3)), sem((6, 2, 4)), sem((7, 3)), sem((7, 4)),
     ]
 
     def body(queries, keys, values, student_x, student_bc, student_dt, a_log, dt_bias, skip):
         whole = pl.BlockSpec(memory_space=pltpu.VMEM)
+        far = pl.BlockSpec(memory_space=pltpu.HBM)
 
         def run(*refs):
             kernel(entries, dp_size, tensor_size, *refs)
@@ -681,11 +742,11 @@
                 jax.ShapeDtypeStruct((HG, 128), F32),
                 jax.ShapeDtypeStruct((8, 128), F32),
             ),
-            in_specs=[whole] * 9,
+            in_specs=[far] * 6 + [whole] * 3,
             out_specs=(whole,) * 5,
             scratch_shapes=scratch,
             compiler_params=pltpu.CompilerParams(
-                collective_id=0, has_side_effects=True, vmem_limit_bytes=60 * 1024 * 1024
+                collective_id=0, has_side_effects=True, vmem_limit_bytes=61 * 1024 * 1024
             ),
             name="align",
         )(
@@ -693,12 +754,26 @@
             student_x.reshape(T, CH), student_bc.reshape(2 * T, N),
             student_dt.reshape(T, HG).T, a_log, dt_bias, skip,
         )
+        gx, gbc, gdt, ghd, gls = pl.pallas_call(
+            write_out,
+            out_shape=(
+                jax.ShapeDtypeStruct((T, CH), BF16),
+                jax.ShapeDtypeStruct((2 * T, N), BF16),
+                jax.ShapeDtypeStruct((HG, T), F32),
+                jax.ShapeDtypeStruct((3, 1, HG), F32),
+                jax.ShapeDtypeStruct((1, 1), F32),
+            ),
+            in_specs=[whole] * 5,
+            out_specs=(whole,) * 5,
+            compiler_params=pltpu.CompilerParams(vmem_limit_bytes=61 * 1024 * 1024),
+            name="write_out",
+        )(gx, gbc, gdt, ghd, gls)
         return (
             gx.reshape(1, T, 1, CH),
             gbc.reshape(1, T, 1, 2, N),
             gdt.T.reshape(1, T, 1, HG),
-            ghd[:, :3].T.reshape(3, 1, HG),
-            gls[0, 0],
+            ghd,
+            gls.reshape(()),
         )
 
     return jax.shard_map(

time: 104 us -> 80.7 us (0.78)
  Pallas kernels: 97 us -> 80 us
  local copies, waits for them, and re-layouts: 5.74 us -> 0 us
    pallas_call x1, Pallas kernels: 97 us -> 78 us  [body(): pl.pallas_call(run, out_shape=(jax.ShapeDtypeStruct((T, CH), BF16), jax.S...]
    unnamed x10 -> x0, local copies, waits for them, and re-layouts: 4.56 us -> none
    pallas_call x0 -> x1, Pallas kernels: none -> 1.99 us  [body(): pl.pallas_call(write_out, out_shape=(jax.ShapeDtypeStruct((T, CH), BF16),...]
    slice x1 -> x0, local copies, waits for them, and re-layouts: 1.17 us -> none  [body(): gls[0, 0]]
where the time goes in v1:
time: 80.7 us; the launch traced here: 80.6 us
  Pallas kernels  80 us (99%)
    pallas_call x1, Pallas kernels, body(): pl.pallas_call(run, out_shape=(jax.ShapeDtypeStruct((T, CH), BF16), jax.S...  78 us
    pallas_call x1, Pallas kernels, body(): pl.pallas_call(write_out, out_shape=(jax.ShapeDtypeStruct((T, CH), BF16),...  1.99 us

profile of v1, /device:TPU:32, one launch (start us, length us, event | category | flops | bytes accessed | tf_op | source)
XLA Modules:
  0.0 80.6 jit_solution(5643199986385299629)
XLA Ops:
  0.6 78.0 %align.1 = (bf16[256,1024]{1,0:T(8,128)(2,1)}, bf16[512,128]{1,0:T(8,128)(2,1)}, f32[16,256]{1,0:T(8,128)}, f32[16,128]{1,0:T(8,128)}, f32[8,128]{1,0:T(8,128)}) custom-call(bf16[256,1024]{1,0:T(8,128)(2,1)} %bitcast.16, bf16[256,128]{1,0:T(8,128)(2,1)} %bitcast.19, bf16[256,128]{1,0:T(8,128)(2,1)} %bitcast.20, bf16[256,1024]{1,0:T(8,128)(2,1)} %bitcast.17, ...), custom_call_target="tpu_custom_call" | custom-call | tf_op jit(solution)/shard_map/align/pallas_call | solution.py:736
  78.6 2.0 %write_out.1 = (bf16[256,1024]{1,0:T(8,128)(2,1)}, bf16[512,128]{1,0:T(8,128)(2,1)}, f32[16,256]{1,0:T(8,128)}, f32[3,1,16]{2,1,0:T(1,128)}, f32[1,1]{1,0:T(1,128)}) custom-call(bf16[256,1024]{1,0:T(8,128)(2,1)} %get-tuple-element.15.gx, bf16[512,128]{1,0:T(8,128)(2,1)} %get-tuple-element.16.gbc, f32[16,256]{1,0:T(8,128)} %get-tuple-element.17.gdt, ...), custom_call_target="tpu_custom_call" | custom-call | tf_op jit(solution)/shard_map/write_out/pallas_call | solution.py:757

commit v2 on v1

--- a/solution.py
+++ b/solution.py
@@ -71,12 +71,12 @@
     gx, gbc, gdt, ghd, gls,
     q, x, bc, dt, kbuf, vbuf, m_ref, acc, timed, mixt, cumb, stepb, cumt, stept, wmat, wtmat,
     intra, inter, upb, ups, ts_full, ecum_full, xs, eu, t1,
-    tot, tq, before,
+    tot, tq, gq, before, weight_z, weight_y, eu_like, zysend, zyrecv,
     ysend, yrecv, zsend, zrecv, bsend, brecv,
     ysend2, yrecv2, zsend2, zrecv2, bsend2, brecv2,
     sy, sz, sd, st, hy, hz, hd,
     own_sem, kv_recv, kvz_send, kvy_send,
-    tot_send, tot_recv, scan_send, scan_recv, red_send, red_recv,
+    tot_send, tot_recv, scan_send, scan_recv, red_send, red_recv, zy_send, zy_recv,
 ):
     c = lax.axis_index("ctx")
     d = lax.axis_index("dp")
@@ -219,10 +219,23 @@
     b_cols = b_f.T.astype(BF16)
     c_cols = c_f.T.astype(BF16)
 
-    tot[pl.ds(c, 1)] = jnp.broadcast_to(
-        jnp.concatenate([cum_c[T - 1 : T, :], jnp.zeros((1, 128 - HG), F32)], axis=1)[None],
-        (1, 8, 128),
+    gate = 1.0 / (1.0 + jnp.exp(-shifted))
+    later_than = marks((T, T), lambda s, t: s > t)
+    gate_after = summed(nn, gate, later_than)
+    gate_sum = jnp.broadcast_to(jnp.sum(gate, axis=1, keepdims=True) * rate, (HG, 128))
+    gate_row = jnp.sum(
+        jnp.where(iota((HG, 128), 1) == iota((HG, 128), 0) + HG, gate_sum, 0.0),
+        axis=0, keepdims=True,
     )
+    total_row = jnp.sum(
+        jnp.where(
+            iota((HG, 128), 1) == iota((HG, 128), 0), jnp.broadcast_to(total, (HG, 128)), 0.0
+        ),
+        axis=0, keepdims=True,
+    )
+    tot[pl.ds(c, 1)] = jnp.broadcast_to((total_row + gate_row)[None], (1, 8, 128))
+    weight_z[...] = tail_step * (total - cum_t)
+    weight_y[...] = tail_step * (gate / step_size - rate * gate_after)
     for sub in range(2):
         for part in range(4):
             ysend[sub, part] = nn(b_cols, xs[:, group_cut(part, sub)]).astype(BF16)
@@ -329,13 +342,13 @@
         intra[:, lanes(pair, 128)] = result
         return carry
 
-    lax.fori_loop(0, GROUP // 2, mix_pair, 0)
-    pass_on(0)
 
     @pl.when(z >= 1)
     def _():
         pass_down(1)
 
+    pass_on(0)
+    lax.fori_loop(0, GROUP // 2, mix_pair, 0)
     for step in range(1, ROW):
         tot_y_wait(step)
     for step in range(1, ROW):
@@ -346,9 +359,12 @@
     del tot_all_ready
     totals = jnp.sum(jnp.where(iota((16, 8, 128), 1) == 0, tot[...], 0.0), axis=1)
     mine = marks((128, QW), lambda h, j: h == y * 4 + (j >> 6))
+    mine_next = marks((128, QW), lambda h, j: h == HG + y * 4 + (j >> 6))
     here = summed(nn, totals, mine)
+    here_next = summed(nn, totals, mine_next)
     for sub in range(2):
         tq[sub] = here[:, sub * 128 : (sub + 1) * 128]
+        gq[sub] = here_next[:, sub * 128 : (sub + 1) * 128]
 
     def total_of(sub, zz, kk):
         return tq[sub, pl.ds(zz * ROW + kk, 1), :]
@@ -376,6 +392,21 @@
             back[sub, kk] = (jnp.exp(passed) * held + pre[sub, kk]).astype(BF16)
             passed = passed + total_of(sub, z, kk)
         trades(phase, sub, back, final)
+
+    def tiles(a):
+        return jnp.sum(a.reshape(N // 8, 8, 128), axis=0)
+
+    def functionals(sub):
+        for_decay = jnp.zeros((8, 128), F32)
+        for_shift = jnp.zeros((8, 128), F32)
+        for kk in range(ROW):
+            later = bsend2[sub, kk].astype(F32)
+            sofar = total_of(sub, z, kk)
+            met = jnp.exp(sofar) * tiles(later * bsend[sub, kk].astype(F32))
+            gates = gq[sub, pl.ds(z * ROW + kk, 1), :]
+            for_decay = for_decay + tiles(later * zyrecv[kk, 2 * sub].astype(F32)) + sofar * met
+            for_shift = for_shift + tiles(later * zyrecv[kk, 2 * sub + 1].astype(F32)) - gates * met
+        return for_decay, for_shift
 
     ahead = (0, 1, 2, 3)
     behind = (3, 2, 1, 0)
@@ -421,26 +452,37 @@
 
     all_heads = (0, 1, GROUP)
     loads[3].wait()
-    settle(0)
-    attend(z, True, (0, 2, GROUP // 2))
 
     @pl.when(z >= 2)
     def _():
         pass_down(2)
 
+    @pl.when(z >= 3)
+    def _():
+        pass_down(3)
+
+    settle(0)
+    attend(z, True, (0, 2, GROUP // 2))
+
     @pl.when(z >= 1)
     def _():
         pass_on(1)
 
-    @pl.when(z >= 3)
-    def _():
-        pass_down(3)
-
     attend(z, True, (1, 2, GROUP // 2))
 
     @pl.when(z >= 2)
     def _():
         pass_on(2)
+        settle(1)
+        attend(z - 1, False, (0, 2, GROUP // 2))
+
+    @pl.when(z >= 3)
+    def _():
+        pass_on(3)
+
+    @pl.when(z >= 2)
+    def _():
+        attend(z - 1, False, (1, 2, GROUP // 2))
 
     for sub in range(2):
         for step in range(1, ROW):
@@ -451,14 +493,8 @@
 
         scan_back(2, sub, zrecv, bsend, brecv, before, ahead, (0, 1, 2), lambda zz: zz < z)
 
-    @pl.when(z >= 2)
-    def _():
-        settle(1)
-        attend(z - 1, False, all_heads)
-
     @pl.when(z >= 3)
     def _():
-        pass_on(3)
         settle(2)
         attend(z - 2, False, all_heads)
 
@@ -482,6 +518,14 @@
         for j in range(1, a.shape[1] // 128):
             out = out + a[:, j * 128 : (j + 1) * 128]
         return out
+
+    def rise(sub):
+        scan_row(3, sub, ysend2, yrecv2, zsend2, before, behind)
+        for step in range(1, ROW):
+
+            @pl.when(z >= step)
+            def _():
+                climb(4, sub, zsend2, zrecv2, ROW - step).start()
 
     power = jnp.zeros((8, 128), F32)
     error = jnp.zeros((8, 128), F32)
@@ -534,17 +578,34 @@
         for copy in spread_out(buf, place, stage, at, size):
             copy.start()
 
-    launch(jnp.concatenate([power, error], axis=0), sy, y, 0, at_y, ROW)
-
-    for sub in range(2):
-        scan_row(3, sub, ysend2, yrecv2, zsend2, before, behind)
-        for step in range(1, ROW):
-
-            @pl.when(z >= step)
-            def _():
-                climb(4, sub, zsend2, zrecv2, ROW - step).start()
-
-    launch(collect(sy, y, 0, at_y, ROW), sz, z, 1, at_z, ROW)
+    launch(jnp.concatenate([power, error], axis=0), sd, d, 2, at_d, dp_size)
+    for kind, weight in enumerate((weight_z, weight_y)):
+        eu_like[...] = (summed(tn, weight[...], spread, 2) * x[...].astype(F32)).astype(BF16)
+        for sub in range(2):
+            for part in range(4):
+                zysend[part, 2 * sub + kind] = nn(
+                    b_cols, eu_like[:, group_cut(part, sub)]
+                ).astype(BF16)
+
+    def zy(step):
+        to = (y + step) % ROW
+        return remote(
+            zysend.at[to], zyrecv.at[y], zy_send.at[step - 1], zy_recv.at[y], at_y(step)
+        )
+
+    def zy_wait(step):
+        other = (y + step) % ROW
+        remote(
+            zysend.at[other], zyrecv.at[other], zy_send.at[step - 1], zy_recv.at[other], at_y(step)
+        ).wait_recv()
+
+    for step in range(1, ROW):
+        zy(step).start()
+    zyrecv[pl.ds(y, 1)] = zysend[pl.ds(y, 1)]
+    launch(collect(sd, d, 2, at_d, dp_size), st, tt, 3, at_t, tensor_size)
+
+    rise(0)
+    rise(1)
 
     def pair_products(pair, running):
         ups_pair = halves(upb[:, lanes(pair, 128)])
@@ -557,26 +618,8 @@
         t1[:, lanes(pair, 128)] = through
         return running
 
-    paired = lax.fori_loop(0, GROUP // 2, pair_products, jnp.zeros((T, T), F32))
-    launch(collect(sz, z, 1, at_z, ROW), sd, d, 2, at_d, dp_size)
-    paired = lax.fori_loop(GROUP // 2, GROUP, pair_products, paired)
-    for sub in range(2):
-        for step in range(1, ROW):
-
-            @pl.when(z + step < ROW)
-            def _():
-                climb_wait(4, sub, zsend2, zrecv2, step)
-
-        scan_back(5, sub, zrecv2, bsend2, brecv2, before, behind, (3, 2, 1), lambda zz: zz > z)
-    launch(collect(sd, d, 2, at_d, dp_size), st, tt, 3, at_t, tensor_size)
-
-    paired_rows = paired.astype(BF16)
-    paired_cols = paired.T.astype(BF16)
-    grad_b = nn(paired_cols, c_rows)
-    grad_c = nn(paired_rows, b_rows)
-    for sub in range(2):
-        for part in range(4):
-            grad_c = grad_c + nt(eu[:, group_cut(part, sub)], brecv[sub, part])
+    paired = lax.fori_loop(0, GROUP, pair_products, jnp.zeros((T, T), F32), unroll=2)
+    launch(collect(st, tt, 3, at_t, tensor_size), sy, y, 0, at_y, ROW)
 
     def by_head(a):
         return summed(nt, a, spread, 2, left=False)
@@ -595,9 +638,46 @@
     since = marks((T, T), lambda s, t: s >= t)
     until = marks((T, T), lambda s, t: s < t)
     gained_after = summed(nn, gained, since)
-    gate = 1.0 / (1.0 + jnp.exp(-shifted))
-
-    both_sums = collect(st, tt, 3, at_t, tensor_size)
+    decay_local = jnp.sum(gained_after * decay, axis=1, keepdims=True)
+    shift_local = jnp.sum(
+        (from_mix / step_size - gained_after * rate) * gate, axis=1, keepdims=True
+    )
+    launch(collect(sy, y, 0, at_y, ROW), sz, z, 1, at_z, ROW)
+
+    for step in range(1, ROW):
+        zy_wait(step)
+    parts = []
+    for sub in range(2):
+        for step in range(1, ROW):
+
+            @pl.when(z + step < ROW)
+            def _():
+                climb_wait(4, sub, zsend2, zrecv2, step)
+
+        scan_back(5, sub, zrecv2, bsend2, brecv2, before, behind, (3, 2, 1), lambda zz: zz > z)
+        parts.append(functionals(sub))
+    owned = marks((HG, QW), lambda h, j: h == y * 4 + (j >> 6))
+
+    def owned_heads(kind):
+        both = jnp.concatenate([parts[0][kind], parts[1][kind]], axis=1)
+        return jnp.sum(summed(nt, both, owned, left=False), axis=1, keepdims=True)
+
+    lane = iota((HG, 128), 1)
+    heads = jnp.where(
+        lane == 0, decay_local + owned_heads(0),
+        jnp.where(lane == 1, shift_local + owned_heads(1), skip_term),
+    )
+    launch(heads, hd, d, 6, at_d, dp_size)
+
+    paired_rows = paired.astype(BF16)
+    paired_cols = paired.T.astype(BF16)
+    grad_b = nn(paired_cols, c_rows)
+    grad_c = nn(paired_rows, b_rows)
+    for sub in range(2):
+        for part in range(4):
+            grad_c = grad_c + nt(eu[:, group_cut(part, sub)], brecv[sub, part])
+
+    both_sums = collect(sz, z, 1, at_z, ROW)
     power_all = jnp.sum(both_sums[0:8, :], keepdims=True)
     error_all = jnp.sum(both_sums[8:16, :], keepdims=True)
     mean_square = power_all / entries + EPSILON
@@ -613,35 +693,30 @@
             cut = group_cut(part, sub)
             later = brecv2[sub, part]
             came = ts_full[:, cut] * nn(b_rows, later)
-            inter[:, cut] = came
+            gx[:, cut] = (
+                (skip_row[:, cut] * ups[:, cut] + t1[:, cut] + came) * factor
+            ).astype(BF16)
+            grad_b = grad_b + nt(xs[:, cut], later)
             later_stats = later_stats + nn(
                 (x[:, cut].astype(F32) * came).astype(BF16), heads_at[cut, :]
             )
             prod = later.astype(F32) * brecv[sub, part].astype(F32)
-            overlap[2 * part + sub] = jnp.sum(prod.reshape(N // 8, 8, 128), axis=0)
+            overlap[2 * part + sub] = tiles(prod)
+        if sub == 0:
+            launch(collect(hd, d, 6, at_d, dp_size), hz, z, 5, at_z, ROW)
     from_later = later_stats.T[0:HG]
     meet = jnp.sum(by_head(jnp.concatenate(overlap, axis=1)), axis=1, keepdims=True)
     decay_grad = gained_after + summed(nn, from_later, until) + jnp.exp(total) * meet
     direct = (from_mix + from_later) / step_size
     shift_grad = (direct - decay_grad * rate) * gate
-    decay_term = jnp.sum(decay_grad * decay, axis=1, keepdims=True)
-    shift_term = jnp.sum(shift_grad, axis=1, keepdims=True)
-    lane = iota((HG, 128), 1)
-    heads = jnp.where(lane == 0, decay_term, jnp.where(lane == 1, shift_term, skip_term))
-    launch(heads, hy, y, 4, at_y, ROW)
     gdt[...] = shift_grad * factor
-    for sub in range(2):
-        for part in range(4):
-            grad_b = grad_b + nt(xs[:, group_cut(part, sub)], brecv2[sub, part])
-    launch(collect(hy, y, 4, at_y, ROW), hz, z, 5, at_z, ROW)
+    launch(collect(hz, z, 5, at_z, ROW), hy, y, 4, at_y, ROW)
     put_b = marks((2 * T, T), lambda r, t: r == 2 * t)
     put_c = marks((2 * T, T), lambda r, t: r == 2 * t + 1)
     gbc[...] = (
         nn(put_b, (grad_b * factor).astype(BF16)) + nn(put_c, (grad_c * factor).astype(BF16))
     ).astype(BF16)
-    launch(collect(hz, z, 5, at_z, ROW), hd, d, 6, at_d, dp_size)
-    gx[...] = ((skip_row * ups[...] + t1[...] + inter[...]) * factor).astype(BF16)
-    ghd[...] = collect(hd, d, 6, at_d, dp_size) * factor
+    ghd[...] = collect(hy, y, 4, at_y, ROW) * factor
 
     for step in range(1, ROW):
 
@@ -657,6 +732,7 @@
             for sub in range(2):
                 climb(4, sub, zsend2, zrecv2, ROW - step).wait_send()
 
+        zy(step).wait_send()
         tot_y(step).wait_send()
         tot_z(step).wait_send()
         for sub in range(2):
@@ -708,7 +784,9 @@
         vm((T, CH), F32), vm((T, CH), F32), vm((T, CH), BF16), vm((T, CH), F32),
         vm((T, CH), F32), vm((T, CH), F32), vm((T, CH), BF16), vm((T, CH), BF16),
         vm((T, CH), F32),
-        vm((16, 8, 128), F32), vm((2, 16, 128), F32), vm((2, ROW, N, 128), F32),
+        vm((16, 8, 128), F32), vm((2, 16, 128), F32), vm((2, 16, 128), F32), vm((2, ROW, N, 128), F32),
+        vm((HG, T), F32), vm((HG, T), F32), vm((T, CH), BF16),
+        vm((ROW, 4, N, 128), BF16), vm((ROW, 4, N, 128), BF16),
     ]
     for _ in range(2):
         scratch += [
@@ -723,7 +801,7 @@
     sem = pltpu.SemaphoreType.DMA
     scratch += [
         sem((6,)), sem((2, 16)), sem((3, 2)), sem((4, 6)),
-        sem((2, 3)), sem((2, 4)), sem((6, 2, 3)), sem((6, 2, 4)), sem((7, 3)), sem((7, 4)),
+        sem((2, 3)), sem((2, 4)), sem((6, 2, 3)), sem((6, 2, 4)), sem((7, 3)), sem((7, 4)), sem((3,)), sem((4,)),
     ]
 
     def body(queries, keys, values, student_x, student_bc, student_dt, a_log, dt_bias, skip):

time: 80.7 us -> 77.1 us (0.955)
  Pallas kernels: 80 us -> 76 us
    pallas_call x1, Pallas kernels: 78 us -> 74.1 us  [body(): pl.pallas_call(run, out_shape=(jax.ShapeDtypeStruct((T, CH), BF16), jax.S...]
where the time goes in v2:
time: 77.1 us; the launch traced here: 76.7 us
  Pallas kernels  76 us (99%)
    pallas_call x1, Pallas kernels, body(): pl.pallas_call(run, out_shape=(jax.ShapeDtypeStruct((T, CH), BF16), jax.S...  74.1 us
    pallas_call x1, Pallas kernels, body(): pl.pallas_call(write_out, out_shape=(jax.ShapeDtypeStruct((T, CH), BF16),...  1.99 us

profile of v2, /device:TPU:32, one launch (start us, length us, event | category | flops | bytes accessed | tf_op | source)
XLA Modules:
  0.0 76.7 jit_solution(6746501670584430988)
XLA Ops:
  0.6 74.1 %align.1 = (bf16[256,1024]{1,0:T(8,128)(2,1)}, bf16[512,128]{1,0:T(8,128)(2,1)}, f32[16,256]{1,0:T(8,128)}, f32[16,128]{1,0:T(8,128)}, f32[8,128]{1,0:T(8,128)}) custom-call(bf16[256,1024]{1,0:T(8,128)(2,1)} %bitcast.16, bf16[256,128]{1,0:T(8,128)(2,1)} %bitcast.19, bf16[256,128]{1,0:T(8,128)(2,1)} %bitcast.20, bf16[256,1024]{1,0:T(8,128)(2,1)} %bitcast.17, ...), custom_call_target="tpu_custom_call" | custom-call | tf_op jit(solution)/shard_map/align/pallas_call | solution.py:814
  74.7 2.0 %write_out.1 = (bf16[256,1024]{1,0:T(8,128)(2,1)}, bf16[512,128]{1,0:T(8,128)(2,1)}, f32[16,256]{1,0:T(8,128)}, f32[3,1,16]{2,1,0:T(1,128)}, f32[1,1]{1,0:T(1,128)}) custom-call(bf16[256,1024]{1,0:T(8,128)(2,1)} %get-tuple-element.15.gx, bf16[512,128]{1,0:T(8,128)(2,1)} %get-tuple-element.16.gbc, f32[16,256]{1,0:T(8,128)} %get-tuple-element.17.gdt, ...), custom_call_target="tpu_custom_call" | custom-call | tf_op jit(solution)/shard_map/write_out/pallas_call | solution.py:835

commit v3 on v2

--- a/solution.py
+++ b/solution.py
@@ -71,7 +71,7 @@
     gx, gbc, gdt, ghd, gls,
     q, x, bc, dt, kbuf, vbuf, m_ref, acc, timed, mixt, cumb, stepb, cumt, stept, wmat, wtmat,
     intra, inter, upb, ups, ts_full, ecum_full, xs, eu, t1,
-    tot, tq, gq, before, weight_z, weight_y, eu_like, zysend, zyrecv,
+    tot, tq, tqo, gqo, before, weight_z, weight_y, eu_like, zysend, zyrecv,
     ysend, yrecv, zsend, zrecv, bsend, brecv,
     ysend2, yrecv2, zsend2, zrecv2, bsend2, brecv2,
     sy, sz, sd, st, hy, hz, hd,
@@ -158,7 +158,7 @@
     def forwards(back):
         return [kv_y(back, 4, 0, slot_of(back, 3), 1), kv_y(back, 5, 1, slot_of(back, 1), 3)]
 
-    for step in (3, 2, 1):
+    for step in (1, 2, 3):
 
         @pl.when(z + step < ROW)
         def _():
@@ -355,19 +355,23 @@
         tot_z(step).start()
     lax.fori_loop(GROUP // 2, GROUP, mix_pair, 0)
 
-    tot_all_ready = [tot_z_wait(step) for step in range(1, ROW)]
-    del tot_all_ready
-    totals = jnp.sum(jnp.where(iota((16, 8, 128), 1) == 0, tot[...], 0.0), axis=1)
     mine = marks((128, QW), lambda h, j: h == y * 4 + (j >> 6))
     mine_next = marks((128, QW), lambda h, j: h == HG + y * 4 + (j >> 6))
-    here = summed(nn, totals, mine)
-    here_next = summed(nn, totals, mine_next)
-    for sub in range(2):
-        tq[sub] = here[:, sub * 128 : (sub + 1) * 128]
-        gq[sub] = here_next[:, sub * 128 : (sub + 1) * 128]
+    row_tot = jnp.sum(
+        jnp.where(iota((ROW, 8, 128), 1) == 0, tot[pl.ds(z * ROW, ROW)], 0.0), axis=1
+    )
+    row_tot = jnp.concatenate([row_tot, row_tot], axis=0)
+    own_tot = summed(nn, row_tot, mine)
+    own_gate = summed(nn, row_tot, mine_next)
+    for sub in range(2):
+        tqo[sub] = own_tot[:, sub * 128 : (sub + 1) * 128]
+        gqo[sub] = own_gate[:, sub * 128 : (sub + 1) * 128]
+
+    def own_total(sub, kk):
+        return tqo[sub, kk : kk + 1, :]
 
     def total_of(sub, zz, kk):
-        return tq[sub, pl.ds(zz * ROW + kk, 1), :]
+        return tq[sub, zz * ROW + kk : zz * ROW + kk + 1, :]
 
     def row_total(sub, zz):
         return sum(total_of(sub, zz, kk) for kk in range(1, ROW)) + total_of(sub, zz, 0)
@@ -378,7 +382,7 @@
         run = jnp.zeros((N, 128), F32)
         for kk in order:
             pre[sub, kk] = run
-            run = jnp.exp(total_of(sub, z, kk)) * run + got[sub, kk].astype(F32)
+            run = jnp.exp(own_total(sub, kk)) * run + got[sub, kk].astype(F32)
         up[sub] = run.astype(BF16)
 
     def scan_back(phase, sub, got, back, final, pre, order, rows_in, arrived):
@@ -390,7 +394,7 @@
         passed = jnp.zeros((1, 128), F32)
         for kk in order:
             back[sub, kk] = (jnp.exp(passed) * held + pre[sub, kk]).astype(BF16)
-            passed = passed + total_of(sub, z, kk)
+            passed = passed + own_total(sub, kk)
         trades(phase, sub, back, final)
 
     def tiles(a):
@@ -401,9 +405,9 @@
         for_shift = jnp.zeros((8, 128), F32)
         for kk in range(ROW):
             later = bsend2[sub, kk].astype(F32)
-            sofar = total_of(sub, z, kk)
+            sofar = own_total(sub, kk)
             met = jnp.exp(sofar) * tiles(later * bsend[sub, kk].astype(F32))
-            gates = gq[sub, pl.ds(z * ROW + kk, 1), :]
+            gates = gqo[sub, kk : kk + 1, :]
             for_decay = for_decay + tiles(later * zyrecv[kk, 2 * sub].astype(F32)) + sofar * met
             for_shift = for_shift + tiles(later * zyrecv[kk, 2 * sub + 1].astype(F32)) - gates * met
         return for_decay, for_shift
@@ -484,6 +488,13 @@
     def _():
         attend(z - 1, False, (1, 2, GROUP // 2))
 
+    for step in range(1, ROW):
+        tot_z_wait(step)
+    totals = jnp.sum(jnp.where(iota((16, 8, 128), 1) == 0, tot[...], 0.0), axis=1)
+    all_tot = summed(nn, totals, mine)
+    for sub in range(2):
+        tq[sub] = all_tot[:, sub * 128 : (sub + 1) * 128]
+
     for sub in range(2):
         for step in range(1, ROW):
 
@@ -602,10 +613,10 @@
     for step in range(1, ROW):
         zy(step).start()
     zyrecv[pl.ds(y, 1)] = zysend[pl.ds(y, 1)]
-    launch(collect(sd, d, 2, at_d, dp_size), st, tt, 3, at_t, tensor_size)
 
     rise(0)
     rise(1)
+    launch(collect(sd, d, 2, at_d, dp_size), st, tt, 3, at_t, tensor_size)
 
     def pair_products(pair, running):
         ups_pair = halves(upb[:, lanes(pair, 128)])
@@ -619,7 +630,6 @@
         return running
 
     paired = lax.fori_loop(0, GROUP, pair_products, jnp.zeros((T, T), F32), unroll=2)
-    launch(collect(st, tt, 3, at_t, tensor_size), sy, y, 0, at_y, ROW)
 
     def by_head(a):
         return summed(nt, a, spread, 2, left=False)
@@ -642,11 +652,18 @@
     shift_local = jnp.sum(
         (from_mix / step_size - gained_after * rate) * gate, axis=1, keepdims=True
     )
-    launch(collect(sy, y, 0, at_y, ROW), sz, z, 1, at_z, ROW)
+    paired_rows = paired.astype(BF16)
+    paired_cols = paired.T.astype(BF16)
+    grad_b = nn(paired_cols, c_rows)
+    grad_c = nn(paired_rows, b_rows)
+    for sub in range(2):
+        for part in range(4):
+            grad_c = grad_c + nt(eu[:, group_cut(part, sub)], brecv[sub, part])
+
+    launch(collect(st, tt, 3, at_t, tensor_size), sz, z, 1, at_z, ROW)
 
     for step in range(1, ROW):
         zy_wait(step)
-    parts = []
     for sub in range(2):
         for step in range(1, ROW):
 
@@ -655,7 +672,7 @@
                 climb_wait(4, sub, zsend2, zrecv2, step)
 
         scan_back(5, sub, zrecv2, bsend2, brecv2, before, behind, (3, 2, 1), lambda zz: zz > z)
-        parts.append(functionals(sub))
+    parts = [functionals(0), functionals(1)]
     owned = marks((HG, QW), lambda h, j: h == y * 4 + (j >> 6))
 
     def owned_heads(kind):
@@ -669,21 +686,8 @@
     )
     launch(heads, hd, d, 6, at_d, dp_size)
 
-    paired_rows = paired.astype(BF16)
-    paired_cols = paired.T.astype(BF16)
-    grad_b = nn(paired_cols, c_rows)
-    grad_c = nn(paired_rows, b_rows)
-    for sub in range(2):
-        for part in range(4):
-            grad_c = grad_c + nt(eu[:, group_cut(part, sub)], brecv[sub, part])
-
-    both_sums = collect(sz, z, 1, at_z, ROW)
-    power_all = jnp.sum(both_sums[0:8, :], keepdims=True)
-    error_all = jnp.sum(both_sums[8:16, :], keepdims=True)
-    mean_square = power_all / entries + EPSILON
-    factor = 1.0 / mean_square
-    gls[...] = jnp.broadcast_to(error_all / mean_square / entries, (8, 128))
-
+    launch(collect(sz, z, 1, at_z, ROW), sy, y, 0, at_y, ROW)
+    launch(collect(hd, d, 6, at_d, dp_size), hz, z, 5, at_z, ROW)
     overlap = [None] * 8
     later_stats = jnp.zeros((T, 128), F32)
     for sub in range(2):
@@ -693,9 +697,7 @@
             cut = group_cut(part, sub)
             later = brecv2[sub, part]
             came = ts_full[:, cut] * nn(b_rows, later)
-            gx[:, cut] = (
-                (skip_row[:, cut] * ups[:, cut] + t1[:, cut] + came) * factor
-            ).astype(BF16)
+            inter[:, cut] = skip_row[:, cut] * ups[:, cut] + t1[:, cut] + came
             grad_b = grad_b + nt(xs[:, cut], later)
             later_stats = later_stats + nn(
                 (x[:, cut].astype(F32) * came).astype(BF16), heads_at[cut, :]
@@ -703,14 +705,21 @@
             prod = later.astype(F32) * brecv[sub, part].astype(F32)
             overlap[2 * part + sub] = tiles(prod)
         if sub == 0:
-            launch(collect(hd, d, 6, at_d, dp_size), hz, z, 5, at_z, ROW)
+            launch(collect(hz, z, 5, at_z, ROW), hy, y, 4, at_y, ROW)
     from_later = later_stats.T[0:HG]
     meet = jnp.sum(by_head(jnp.concatenate(overlap, axis=1)), axis=1, keepdims=True)
     decay_grad = gained_after + summed(nn, from_later, until) + jnp.exp(total) * meet
     direct = (from_mix + from_later) / step_size
     shift_grad = (direct - decay_grad * rate) * gate
+    both_sums = collect(sy, y, 0, at_y, ROW)
+    power_all = jnp.sum(both_sums[0:8, :], keepdims=True)
+    error_all = jnp.sum(both_sums[8:16, :], keepdims=True)
+    mean_square = power_all / entries + EPSILON
+    factor = 1.0 / mean_square
+    gls[...] = jnp.broadcast_to(error_all / mean_square / entries, (8, 128))
+
+    gx[...] = (inter[...] * factor).astype(BF16)
     gdt[...] = shift_grad * factor
-    launch(collect(hz, z, 5, at_z, ROW), hy, y, 4, at_y, ROW)
     put_b = marks((2 * T, T), lambda r, t: r == 2 * t)
     put_c = marks((2 * T, T), lambda r, t: r == 2 * t + 1)
     gbc[...] = (
@@ -784,7 +793,8 @@
         vm((T, CH), F32), vm((T, CH), F32), vm((T, CH), BF16), vm((T, CH), F32),
         vm((T, CH), F32), vm((T, CH), F32), vm((T, CH), BF16), vm((T, CH), BF16),
         vm((T, CH), F32),
-        vm((16, 8, 128), F32), vm((2, 16, 128), F32), vm((2, 16, 128), F32), vm((2, ROW, N, 128), F32),
+        vm((16, 8, 128), F32), vm((2, 16, 128), F32), vm((2, 8, 128), F32), vm((2, 8, 128), F32),
+        vm((2, ROW, N, 128), F32),
         vm((HG, T), F32), vm((HG, T), F32), vm((T, CH), BF16),
         vm((ROW, 4, N, 128), BF16), vm((ROW, 4, N, 128), BF16),
     ]

time: 77.1 us -> 74.6 us (0.968)
  Pallas kernels: 76 us -> 73.8 us
    pallas_call x1, Pallas kernels: 74.1 us -> 71.8 us  [body(): pl.pallas_call(run, out_shape=(jax.ShapeDtypeStruct((T, CH), BF16), jax.S...]
where the time goes in v3:
time: 74.6 us; the launch traced here: 74.4 us
  Pallas kernels  73.8 us (99%)
    pallas_call x1, Pallas kernels, body(): pl.pallas_call(run, out_shape=(jax.ShapeDtypeStruct((T, CH), BF16), jax.S...  71.8 us
    pallas_call x1, Pallas kernels, body(): pl.pallas_call(write_out, out_shape=(jax.ShapeDtypeStruct((T, CH), BF16),...  1.99 us

profile of v3, /device:TPU:32, one launch (start us, length us, event | category | flops | bytes accessed | tf_op | source)
XLA Modules:
  0.0 74.4 jit_solution(6056287345777000762)
XLA Ops:
  0.6 71.8 %align.1 = (bf16[256,1024]{1,0:T(8,128)(2,1)}, bf16[512,128]{1,0:T(8,128)(2,1)}, f32[16,256]{1,0:T(8,128)}, f32[16,128]{1,0:T(8,128)}, f32[8,128]{1,0:T(8,128)}) custom-call(bf16[256,1024]{1,0:T(8,128)(2,1)} %bitcast.16, bf16[256,128]{1,0:T(8,128)(2,1)} %bitcast.19, bf16[256,128]{1,0:T(8,128)(2,1)} %bitcast.20, bf16[256,1024]{1,0:T(8,128)(2,1)} %bitcast.17, ...), custom_call_target="tpu_custom_call" | custom-call | tf_op jit(solution)/shard_map/align/pallas_call | solution.py:824
  72.4 2.0 %write_out.1 = (bf16[256,1024]{1,0:T(8,128)(2,1)}, bf16[512,128]{1,0:T(8,128)(2,1)}, f32[16,256]{1,0:T(8,128)}, f32[3,1,16]{2,1,0:T(1,128)}, f32[1,1]{1,0:T(1,128)}) custom-call(bf16[256,1024]{1,0:T(8,128)(2,1)} %get-tuple-element.15.gx, bf16[512,128]{1,0:T(8,128)(2,1)} %get-tuple-element.16.gbc, f32[16,256]{1,0:T(8,128)} %get-tuple-element.17.gdt, ...), custom_call_target="tpu_custom_call" | custom-call | tf_op jit(solution)/shard_map/write_out/pallas_call | solution.py:845

commit v4 on v3

--- a/solution.py
+++ b/solution.py
@@ -348,13 +348,17 @@
         pass_down(1)
 
     pass_on(0)
-    lax.fori_loop(0, GROUP // 2, mix_pair, 0)
+    lax.fori_loop(0, GROUP // 2, mix_pair, 0, unroll=2)
     for step in range(1, ROW):
         tot_y_wait(step)
     for step in range(1, ROW):
         tot_z(step).start()
-    lax.fori_loop(GROUP // 2, GROUP, mix_pair, 0)
-
+    lax.fori_loop(GROUP // 2, GROUP, mix_pair, 0, unroll=2)
+
+
+    @pl.when(z >= 2)
+    def _():
+        pass_down(2)
     mine = marks((128, QW), lambda h, j: h == y * 4 + (j >> 6))
     mine_next = marks((128, QW), lambda h, j: h == HG + y * 4 + (j >> 6))
     row_tot = jnp.sum(
@@ -456,10 +460,6 @@
 
     all_heads = (0, 1, GROUP)
     loads[3].wait()
-
-    @pl.when(z >= 2)
-    def _():
-        pass_down(2)
 
     @pl.when(z >= 3)
     def _():

time: 74.6 us -> 73.9 us (level)
  Pallas kernels: 73.8 us -> 73 us
    pallas_call x1, Pallas kernels: 71.8 us -> 71 us  [body(): pl.pallas_call(run, out_shape=(jax.ShapeDtypeStruct((T, CH), BF16), jax.S...]
where the time goes in v4:
time: 73.9 us; the launch traced here: 73.6 us
  Pallas kernels  73 us (99%)
    pallas_call x1, Pallas kernels, body(): pl.pallas_call(run, out_shape=(jax.ShapeDtypeStruct((T, CH), BF16), jax.S...  71 us
    pallas_call x1, Pallas kernels, body(): pl.pallas_call(write_out, out_shape=(jax.ShapeDtypeStruct((T, CH), BF16),...  1.99 us

profile of v4, /device:TPU:32, one launch (start us, length us, event | category | flops | bytes accessed | tf_op | source)
XLA Modules:
  0.0 73.6 jit_solution(8132889526587347390)
XLA Ops:
  0.6 71.0 %align.1 = (bf16[256,1024]{1,0:T(8,128)(2,1)}, bf16[512,128]{1,0:T(8,128)(2,1)}, f32[16,256]{1,0:T(8,128)}, f32[16,128]{1,0:T(8,128)}, f32[8,128]{1,0:T(8,128)}) custom-call(bf16[256,1024]{1,0:T(8,128)(2,1)} %bitcast.16, bf16[256,128]{1,0:T(8,128)(2,1)} %bitcast.19, bf16[256,128]{1,0:T(8,128)(2,1)} %bitcast.20, bf16[256,1024]{1,0:T(8,128)(2,1)} %bitcast.17, ...), custom_call_target="tpu_custom_call" | custom-call | tf_op jit(solution)/shard_map/align/pallas_call | solution.py:824
  71.6 2.0 %write_out.1 = (bf16[256,1024]{1,0:T(8,128)(2,1)}, bf16[512,128]{1,0:T(8,128)(2,1)}, f32[16,256]{1,0:T(8,128)}, f32[3,1,16]{2,1,0:T(1,128)}, f32[1,1]{1,0:T(1,128)}) custom-call(bf16[256,1024]{1,0:T(8,128)(2,1)} %get-tuple-element.15.gx, bf16[512,128]{1,0:T(8,128)(2,1)} %get-tuple-element.16.gbc, f32[16,256]{1,0:T(8,128)} %get-tuple-element.17.gdt, ...), custom_call_target="tpu_custom_call" | custom-call | tf_op jit(solution)/shard_map/write_out/pallas_call | solution.py:845
